TPU v7x, 256 devices: a whole 4x4x8 slice. The times are simulated.
256 devices in a mesh: dom: 64 (over z, y, core), chan: 4 (over x).
Axes of the slice: x: 4, y: 4, z: 8, core: 2. Of those that a mesh axis runs over, the one named last changes fastest.
Arguments:
- features: bfloat16 [256, 65536], P('chan', 'dom'), may hold values from -6 to 6
- cotangent: bfloat16 [256, 65536], P('chan', 'dom'), may hold values from -6 to 6
- weights: bfloat16 [9, 256, 256], P(None, 'chan'), may hold values from -0.375 to 0.375
- tile_values: float32 [4096, 128, 128], P('dom'), may hold values from -0.046875 to 0.046875
- tile_cols: int32 [64, 8, 8], P('dom'), may hold values from 0 to 11, as said below
- send_list: int32 [64, 4, 128], P('dom'), may hold values from 0 to 1023
Outputs:
- input_grad: float32 [256, 65536], P('chan', 'dom')
- weight_grad: float32 [9, 256, 256], P(None, None, 'chan')
Inputs may be any that keep to these rules, and one draw needn't show every extreme that they name: `tile_cols`: values below 8 are blocks of the partition's own nodes; 8 + s is the block received from neighbour slot s. Tile 0 of row block r has column block r.
All inputs are finite; a program needn't handle non-finite values.
Results may differ from a plain program's by a relative error of at most 0.0003.
Values may be sent and summed in bfloat16 or wider, within the bound.
A program may use at most 128 MiB of HBM per device.

v0:
```python
import jax
import jax.numpy as jnp
from jax import lax
from jax.sharding import PartitionSpec as P

NEIGHBOUR_SHIFTS = (1, -1, 2, -2)


def from_behind(block, axis, distance):
    devices = range(lax.axis_size(axis))
    route = [((i - distance) % len(devices), i) for i in devices]
    return lax.ppermute(block, axis, route)


def exchange_rows(outgoing):
    received = [
        from_behind(outgoing[:, slot_index], "dom", offset)
        for slot_index, offset in enumerate(NEIGHBOUR_SHIFTS)
    ]
    return received


def apply_operator(field_in, tile_values, tile_cols, send_list):
    channels, local_nodes = field_in.shape
    tile_size = tile_values.shape[-1]
    per_row = tile_cols.shape[-1]
    outgoing = jnp.take(field_in, send_list[0], axis=1)
    received = exchange_rows(outgoing)
    extended = jnp.concatenate([field_in] + received, axis=1)
    blocks = extended.reshape(channels, -1, tile_size)
    picked = jnp.take(blocks, tile_cols.reshape(-1), axis=1)
    product = jnp.einsum("ctj,tjk->ctk", picked, tile_values, precision=lax.Precision.HIGHEST)
    return (
        product.reshape(channels, -1, per_row, tile_size).sum(axis=2).reshape(channels, local_nodes)
    )


def local(features, cotangent, weights, tile_values, tile_cols, send_list):
    top_order = weights.shape[0] - 1
    local_nodes = features.shape[1]

    def operator_on(field_in):
        return apply_operator(field_in, tile_values, tile_cols, send_list)

    feat_all, cot_all = (
        lax.all_gather(features, "chan", axis=0, tiled=True),
        lax.all_gather(cotangent, "chan", axis=0, tiled=True),
    )
    feat_wide = feat_all.astype(jnp.float32)

    def mixed_term(order_index):
        return jnp.dot(weights[order_index], cot_all, preferred_element_type=jnp.float32)

    def grad_term(state):
        return lax.dot_general(
            feat_wide, state, (((1,), (1,)), ((), ())), precision=lax.Precision.HIGHEST
        )

    cheb_prev = cotangent.astype(jnp.float32)
    grad_terms = [grad_term(cheb_prev)]
    cheb_now = operator_on(cheb_prev)
    grad_terms.append(grad_term(cheb_now))
    for order_index in range(2, top_order + 1):
        cheb_prev, cheb_now = (cheb_now, 2.0 * operator_on(cheb_now) - cheb_prev)
        grad_terms.append(grad_term(cheb_now))
    current = mixed_term(top_order)
    clen_later = jnp.zeros_like(current)
    for order_index in range(top_order - 1, 0, -1):
        current, clen_later = (
            mixed_term(order_index) + 2.0 * operator_on(current) - clen_later,
            current,
        )
    input_grad = mixed_term(0) + operator_on(current) - clen_later
    local_grads = jnp.stack(grad_terms)
    summed = lax.psum(local_grads, "dom")
    nodes_all = lax.axis_size("dom") * local_nodes
    return (input_grad, summed * float(nodes_all) ** (-0.5))


def solution(mesh):
    placed = (
        P("chan", "dom"),
        P("chan", "dom"),
        P(None, "chan", None),
        P("dom", None, None),
        P("dom", None, None),
        P("dom", None, None),
    )
    return jax.shard_map(
        local,
        mesh=mesh,
        in_specs=placed,
        out_specs=(P("chan", "dom"), P(None, None, "chan")),
        check_vma=False,
    )
```

profile of v0, /device:TPU:2, one launch (start us, length us, event | category | flops | bytes accessed | tf_op | source)
XLA Modules:
  0.0 664.3 jit_solution(9862079954037837758)
XLA Ops:
  8.6 13.7 %all_gather.6 = bf16[256,1024]{1,0:T(8,128)(2,1)S(1)} all-gather(bf16[64,1024]{1,0:T(8,128)(2,1)} %param.11), channel_id=1, replica_groups=mesh['dom'=64,'chan'=4] {'chan'}, dimensions={0}, use_global_device_ids=true | all-gather | bytes 655360 | tf_op jit(solution)/shard_map/all_gather | solution.py:47
  38.1 12.8 %all_gather.7 = bf16[256,1024]{1,0:T(8,128)(2,1)S(1)} all-gather(bf16[64,1024]{1,0:T(8,128)(2,1)S(1)} %copy-done.13), channel_id=1, replica_groups=mesh['dom'=64,'chan'=4] {'chan'}, dimensions={0}, use_global_device_ids=true | all-gather | bytes 655360 | tf_op jit(solution)/shard_map/all_gather | solution.py:46
  57.3 7.7 %collective-permute-done.34 = f32[64,128]{0,1:T(8,128)S(1)} collective-permute-done((f32[64,128]{0,1:T(8,128)S(1)}, f32[64,128]{0,1:T(8,128)S(1)}, u32[]{:S(2)}, u32[]{:S(2)}) %collective-permute-start.34) | collective-permute-done | bytes 32800 | tf_op jit(solution)/shard_map/ppermute | solution.py:12
  70.4 6.4 bitcast_reduce_fusion.7
  88.4 6.7 %bitcast_reduce_fusion.15 = f32[64,8,128]{2,0,1:T(8,128)S(1)} fusion(f32[64,128,128]{2,1,0:T(8,128)} %param.13, f32[64,64,128]{2,1,0:T(8,128)} %gather_fusion.1, pred[64]{0:T(512)(128)(4,1)S(1)} %compare_and_fusion), kind=kOutput, calls=%fused_computation.47 | convolution fusion | flops 806289408 | bytes 6553664 | tf_op jit(solution)/shard_map/ctj,tjk->ctk/dot_general | solution.py:32
  110.1 5.5 collective-permute-start.37
  123.1 6.7 %bitcast_reduce_fusion.14 = f32[64,8,128]{2,0,1:T(8,128)S(1)} fusion(f32[64,128,128]{2,1,0:T(8,128)} %param.13, f32[64,64,128]{2,1,0:T(8,128)} %gather_fusion.3, pred[64]{0:T(512)(128)(4,1)S(1)} %compare_and_fusion), kind=kOutput, calls=%fused_computation.46 | convolution fusion | flops 806289408 | bytes 6553664 | tf_op jit(solution)/shard_map/ctj,tjk->ctk/dot_general | solution.py:32
  140.8 5.5 collective-permute-start.11
  152.7 6.7 %bitcast_reduce_fusion.6 = f32[64,8,128]{2,0,1:T(8,128)S(1)} fusion(f32[64,128,128]{2,1,0:T(8,128)} %param.13, f32[64,64,128]{2,1,0:T(8,128)} %gather_fusion.19, pred[64]{0:T(512)(128)(4,1)S(1)} %compare_and_fusion), kind=kOutput, calls=%fused_computation.38 | convolution fusion | flops 806289408 | bytes 6553664 | tf_op jit(solution)/shard_map/ctj,tjk->ctk/dot_general | solution.py:32
  172.1 5.5 collective-permute-start.43
  179.7 6.7 %bitcast_reduce_fusion.13 = f32[64,8,128]{2,0,1:T(8,128)S(1)} fusion(f32[64,128,128]{2,1,0:T(8,128)} %param.13, f32[64,64,128]{2,1,0:T(8,128)} %gather_fusion.5, pred[64]{0:T(512)(128)(4,1)S(1)} %compare_and_fusion), kind=kOutput, calls=%fused_computation.45 | convolution fusion | flops 806289408 | bytes 6553664 | tf_op jit(solution)/shard_map/ctj,tjk->ctk/dot_general | solution.py:32
  198.1 5.6 collective-permute-start.15
  210.0 6.7 %bitcast_reduce_fusion.5 = f32[64,8,128]{2,0,1:T(8,128)S(1)} fusion(f32[64,128,128]{2,1,0:T(8,128)} %param.13, f32[64,64,128]{2,1,0:T(8,128)} %gather_fusion.21, pred[64]{0:T(512)(128)(4,1)S(1)} %compare_and_fusion), kind=kOutput, calls=%fused_computation.37 | convolution fusion | flops 806289408 | bytes 6553664 | tf_op jit(solution)/shard_map/ctj,tjk->ctk/dot_general | solution.py:32
  230.5 5.8 collective-permute-start.47
  242.1 6.7 %bitcast_reduce_fusion.12 = f32[64,8,128]{2,0,1:T(8,128)S(1)} fusion(f32[64,128,128]{2,1,0:T(8,128)} %param.13, f32[64,64,128]{2,1,0:T(8,128)} %gather_fusion.7, pred[64]{0:T(512)(128)(4,1)S(1)} %compare_and_fusion), kind=kOutput, calls=%fused_computation.44 | convolution fusion | flops 806289408 | bytes 6553664 | tf_op jit(solution)/shard_map/ctj,tjk->ctk/dot_general | solution.py:32
  259.7 5.5 collective-permute-start.19
  270.7 6.7 %bitcast_reduce_fusion.4 = f32[64,8,128]{2,0,1:T(8,128)S(1)} fusion(f32[64,128,128]{2,1,0:T(8,128)} %param.13, f32[64,64,128]{2,1,0:T(8,128)} %gather_fusion.23, pred[64]{0:T(512)(128)(4,1)S(1)} %compare_and_fusion), kind=kOutput, calls=%fused_computation.36 | convolution fusion | flops 806289408 | bytes 6553664 | tf_op jit(solution)/shard_map/ctj,tjk->ctk/dot_general | solution.py:32
  288.3 5.5 collective-permute-start.51
  297.4 6.7 %bitcast_reduce_fusion.11 = f32[64,8,128]{2,0,1:T(8,128)S(1)} fusion(f32[64,128,128]{2,1,0:T(8,128)} %param.13, f32[64,64,128]{2,1,0:T(8,128)} %gather_fusion.9, pred[64]{0:T(512)(128)(4,1)S(1)} %compare_and_fusion), kind=kOutput, calls=%fused_computation.43 | convolution fusion | flops 806289408 | bytes 6553664 | tf_op jit(solution)/shard_map/ctj,tjk->ctk/dot_general | solution.py:32
  314.4 5.6 collective-permute-start.23
  325.5 6.7 %bitcast_reduce_fusion.3 = f32[64,8,128]{2,0,1:T(8,128)S(1)} fusion(f32[64,128,128]{2,1,0:T(8,128)} %param.13, f32[64,64,128]{2,1,0:T(8,128)} %gather_fusion.25, pred[64]{0:T(512)(128)(4,1)S(1)} %compare_and_fusion), kind=kOutput, calls=%fused_computation.35 | convolution fusion | flops 806289408 | bytes 6553664 | tf_op jit(solution)/shard_map/ctj,tjk->ctk/dot_general | solution.py:32
  341.6 5.8 collective-permute-start.55
  349.5 6.7 %bitcast_reduce_fusion.10 = f32[64,8,128]{2,0,1:T(8,128)S(1)} fusion(f32[64,128,128]{2,1,0:T(8,128)} %param.13, f32[64,64,128]{2,1,0:T(8,128)} %gather_fusion.11, pred[64]{0:T(512)(128)(4,1)S(1)} %compare_and_fusion), kind=kOutput, calls=%fused_computation.42 | convolution fusion | flops 806289408 | bytes 6553664 | tf_op jit(solution)/shard_map/ctj,tjk->ctk/dot_general | solution.py:32
  378.1 6.7 %bitcast_reduce_fusion.2 = f32[64,8,128]{2,0,1:T(8,128)S(1)} fusion(f32[64,128,128]{2,1,0:T(8,128)} %param.13, f32[64,64,128]{2,1,0:T(8,128)} %gather_fusion.27, pred[64]{0:T(512)(128)(4,1)S(1)} %compare_and_fusion), kind=kOutput, calls=%fused_computation.34 | convolution fusion | flops 806289408 | bytes 6553664 | tf_op jit(solution)/shard_map/ctj,tjk->ctk/dot_general | solution.py:32
  395.6 5.5 collective-permute-start.59
  404.7 6.7 %bitcast_reduce_fusion.9 = f32[64,8,128]{2,0,1:T(8,128)S(1)} fusion(f32[64,128,128]{2,1,0:T(8,128)} %param.13, f32[64,64,128]{2,1,0:T(8,128)} %gather_fusion.13, pred[64]{0:T(512)(128)(4,1)S(1)} %compare_and_fusion), kind=kOutput, calls=%fused_computation.41 | convolution fusion | flops 806289408 | bytes 6553664 | tf_op jit(solution)/shard_map/ctj,tjk->ctk/dot_general | solution.py:32
  422.4 5.6 collective-permute-start.31
  433.5 6.7 %bitcast_reduce_fusion.1 = f32[64,8,128]{2,0,1:T(8,128)S(1)} fusion(f32[64,128,128]{2,1,0:T(8,128)} %param.13, f32[64,64,128]{2,1,0:T(8,128)} %gather_fusion.29, pred[64]{0:T(512)(128)(4,1)S(1)} %compare_and_fusion), kind=kOutput, calls=%fused_computation.33 | convolution fusion | flops 806289408 | bytes 6553664 | tf_op jit(solution)/shard_map/ctj,tjk->ctk/dot_general | solution.py:32
  450.4 5.6 collective-permute-start.63
  465.5 6.7 %bitcast_reduce_fusion = f32[64,8,128]{2,0,1:T(8,128)S(1)} fusion(f32[64,128,128]{2,1,0:T(8,128)} %param.13, f32[64,64,128]{2,1,0:T(8,128)} %gather_fusion.31, pred[64]{0:T(512)(128)(4,1)S(1)} %compare_and_fusion), kind=kOutput, calls=%fused_computation.32 | convolution fusion | flops 806289408 | bytes 6553664 | tf_op jit(solution)/shard_map/ctj,tjk->ctk/dot_general | solution.py:32
  473.8 6.7 %bitcast_reduce_fusion.8 = f32[64,8,128]{2,0,1:T(8,128)S(1)} fusion(f32[64,128,128]{2,1,0:T(8,128)} %param.13, f32[64,64,128]{2,1,0:T(8,128)} %gather_fusion.15, pred[64]{0:T(512)(128)(4,1)S(1)} %compare_and_fusion), kind=kOutput, calls=%fused_computation.40 | convolution fusion | flops 806289408 | bytes 6553664 | tf_op jit(solution)/shard_map/ctj,tjk->ctk/dot_general | solution.py:32
  482.2 172.9 %all-reduce.2.cloned.1.call-done = f32[9,256,64]{1,2,0:T(8,128)} async-done(((f32[9,256,64]{1,2,0:T(8,128)}), f32[9,256,64]{1,2,0:T(8,128)}) %all-reduce.2.cloned.1.call-update) | async-done | bytes 589840 | tf_op jit(solution)/shard_map/psum | solution.py:75
  (360 shorter events, 267.7 us)
Async XLA Ops:
  7.2 647.9 %all-reduce.2.cloned.1.call-start = ((), (), s32[]{:S(2)}) async-start(), calls=%async_computation | async-start | bytes 1179648 | tf_op jit(solution)/shard_map/psum | solution.py:75
  26.1 52.7 %collective-permute-start = (f32[64,128]{1,0:T(8,128)}, f32[64,128]{1,0:T(8,128)}, u32[]{:S(2)}, u32[]{:S(2)}) collective-permute-start(f32[64,128]{1,0:T(8,128)} %get-tuple-element.67), channel_id=1, source_target_pairs={{252,0},{0,4},{4,8},{8,12},{12,16},{16,20},{20,24},{24,28},{28,32}... | collective-permute-start | bytes 98312 | tf_op jit(solution)/shard_map/ppermute | solution.py:12
  26.1 54.0 %collective-permute-start.1 = (f32[64,128]{1,0:T(8,128)}, f32[64,128]{1,0:T(8,128)}, u32[]{:S(2)}, u32[]{:S(2)}) collective-permute-start(f32[64,128]{1,0:T(8,128)} %get-tuple-element.66), channel_id=1, source_target_pairs={{4,0},{8,4},{12,8},{16,12},{20,16},{24,20},{28,24},{32,28},{36,32}... | collective-permute-start | bytes 98312 | tf_op jit(solution)/shard_map/ppermute | solution.py:12
  31.2 50.4 %collective-permute-start.2 = (f32[64,128]{1,0:T(8,128)}, f32[64,128]{1,0:T(8,128)}, u32[]{:S(2)}, u32[]{:S(2)}) collective-permute-start(f32[64,128]{1,0:T(8,128)} %get-tuple-element.65), channel_id=1, source_target_pairs={{248,0},{252,4},{0,8},{4,12},{8,16},{12,20},{16,24},{20,28},{24,32... | collective-permute-start | bytes 98312 | tf_op jit(solution)/shard_map/ppermute | solution.py:12
  31.2 52.8 %collective-permute-start.3 = (f32[64,128]{1,0:T(8,128)}, f32[64,128]{1,0:T(8,128)}, u32[]{:S(2)}, u32[]{:S(2)}) collective-permute-start(f32[64,128]{1,0:T(8,128)} %get-tuple-element.64), channel_id=1, source_target_pairs={{8,0},{12,4},{16,8},{20,12},{24,16},{28,20},{32,24},{36,28},{40,32... | collective-permute-start | bytes 98312 | tf_op jit(solution)/shard_map/ppermute | solution.py:12
  115.6 32.1 %collective-permute-start.39 = (f32[64,128]{0,1:T(8,128)}, f32[64,128]{0,1:T(8,128)}, u32[]{:S(2)}, u32[]{:S(2)}) collective-permute-start(f32[64,128]{0,1:T(8,128)} %get-tuple-element.28), channel_id=1, source_target_pairs={{8,0},{12,4},{16,8},{20,12},{24,16},{28,20},{32,24},{36,28},{40,32... | collective-permute-start | bytes 98312 | tf_op jit(solution)/shard_map/ppermute | solution.py:12
  132.8 34.2 %collective-permute-start.8 = (f32[64,128]{1,0:T(8,128)}, f32[64,128]{1,0:T(8,128)S(1)}, u32[]{:S(2)}, u32[]{:S(2)}) collective-permute-start(f32[64,128]{1,0:T(8,128)} %get-tuple-element.59), channel_id=1, source_target_pairs={{252,0},{0,4},{4,8},{8,12},{12,16},{16,20},{20,24},{24,28},{28,32}... | collective-permute-start | bytes 98312 | tf_op jit(solution)/shard_map/ppermute | solution.py:12
  132.8 39.2 %collective-permute-start.9 = (f32[64,128]{1,0:T(8,128)}, f32[64,128]{1,0:T(8,128)S(1)}, u32[]{:S(2)}, u32[]{:S(2)}) collective-permute-start(f32[64,128]{1,0:T(8,128)} %get-tuple-element.58), channel_id=1, source_target_pairs={{4,0},{8,4},{12,8},{16,12},{20,16},{24,20},{28,24},{32,28},{36,32}... | collective-permute-start | bytes 98312 | tf_op jit(solution)/shard_map/ppermute | solution.py:12
  139.3 32.7 %collective-permute-start.10 = (f32[64,128]{1,0:T(8,128)}, f32[64,128]{1,0:T(8,128)S(1)}, u32[]{:S(2)}, u32[]{:S(2)}) collective-permute-start(f32[64,128]{1,0:T(8,128)} %get-tuple-element.57), channel_id=1, source_target_pairs={{248,0},{252,4},{0,8},{4,12},{8,16},{12,20},{16,24},{20,28},{24,32... | collective-permute-start | bytes 98312 | tf_op jit(solution)/shard_map/ppermute | solution.py:12
  140.8 36.8 %collective-permute-start.11 = (f32[64,128]{1,0:T(8,128)}, f32[64,128]{1,0:T(8,128)S(1)}, u32[]{:S(2)}, u32[]{:S(2)}) collective-permute-start(f32[64,128]{1,0:T(8,128)} %get-tuple-element.56), channel_id=1, source_target_pairs={{8,0},{12,4},{16,8},{20,12},{24,16},{28,20},{32,24},{36,28},{40,32... | collective-permute-start | bytes 98312 | tf_op jit(solution)/shard_map/ppermute | solution.py:12
  172.1 33.0 %collective-permute-start.43 = (f32[64,128]{0,1:T(8,128)}, f32[64,128]{0,1:T(8,128)}, u32[]{:S(2)}, u32[]{:S(2)}) collective-permute-start(f32[64,128]{0,1:T(8,128)} %get-tuple-element.24), channel_id=1, source_target_pairs={{8,0},{12,4},{16,8},{20,12},{24,16},{28,20},{32,24},{36,28},{40,32... | collective-permute-start | bytes 98312 | tf_op jit(solution)/shard_map/ppermute | solution.py:12
  190.1 32.7 %collective-permute-start.12 = (f32[64,128]{1,0:T(8,128)S(1)}, f32[64,128]{1,0:T(8,128)S(1)}, u32[]{:S(2)}, u32[]{:S(2)}) collective-permute-start(f32[64,128]{1,0:T(8,128)S(1)} %get-tuple-element.55), channel_id=1, source_target_pairs={{252,0},{0,4},{4,8},{8,12},{12,16},{16,20},{20,24},{24,28},{28,32}... | collective-permute-start | bytes 98312 | tf_op jit(solution)/shard_map/ppermute | solution.py:12
  190.1 38.4 %collective-permute-start.13 = (f32[64,128]{1,0:T(8,128)}, f32[64,128]{1,0:T(8,128)S(1)}, u32[]{:S(2)}, u32[]{:S(2)}) collective-permute-start(f32[64,128]{1,0:T(8,128)} %get-tuple-element.54), channel_id=1, source_target_pairs={{4,0},{8,4},{12,8},{16,12},{20,16},{24,20},{28,24},{32,28},{36,32}... | collective-permute-start | bytes 98312 | tf_op jit(solution)/shard_map/ppermute | solution.py:12
  196.6 33.9 %collective-permute-start.14 = (f32[64,128]{1,0:T(8,128)}, f32[64,128]{1,0:T(8,128)}, u32[]{:S(2)}, u32[]{:S(2)}) collective-permute-start(f32[64,128]{1,0:T(8,128)} %get-tuple-element.53), channel_id=1, source_target_pairs={{248,0},{252,4},{0,8},{4,12},{8,16},{12,20},{16,24},{20,28},{24,32... | collective-permute-start | bytes 98312 | tf_op jit(solution)/shard_map/ppermute | solution.py:12
  198.1 39.6 %collective-permute-start.15 = (f32[64,128]{1,0:T(8,128)}, f32[64,128]{1,0:T(8,128)}, u32[]{:S(2)}, u32[]{:S(2)}) collective-permute-start(f32[64,128]{1,0:T(8,128)} %get-tuple-element.52), channel_id=1, source_target_pairs={{8,0},{12,4},{16,8},{20,12},{24,16},{28,20},{32,24},{36,28},{40,32... | collective-permute-start | bytes 98312 | tf_op jit(solution)/shard_map/ppermute | solution.py:12
  222.8 36.3 %collective-permute-start.45 = (f32[64,128]{0,1:T(8,128)}, f32[64,128]{0,1:T(8,128)S(1)}, u32[]{:S(2)}, u32[]{:S(2)}) collective-permute-start(f32[64,128]{0,1:T(8,128)} %get-tuple-element.22), channel_id=1, source_target_pairs={{4,0},{8,4},{12,8},{16,12},{20,16},{24,20},{28,24},{32,28},{36,32}... | collective-permute-start | bytes 98312 | tf_op jit(solution)/shard_map/ppermute | solution.py:12
  229.1 30.6 %collective-permute-start.46 = (f32[64,128]{0,1:T(8,128)}, f32[64,128]{0,1:T(8,128)S(1)}, u32[]{:S(2)}, u32[]{:S(2)}) collective-permute-start(f32[64,128]{0,1:T(8,128)} %get-tuple-element.21), channel_id=1, source_target_pairs={{248,0},{252,4},{0,8},{4,12},{8,16},{12,20},{16,24},{20,28},{24,32... | collective-permute-start | bytes 98312 | tf_op jit(solution)/shard_map/ppermute | solution.py:12
  230.5 35.3 %collective-permute-start.47 = (f32[64,128]{0,1:T(8,128)}, f32[64,128]{0,1:T(8,128)}, u32[]{:S(2)}, u32[]{:S(2)}) collective-permute-start(f32[64,128]{0,1:T(8,128)} %get-tuple-element.20), channel_id=1, source_target_pairs={{8,0},{12,4},{16,8},{20,12},{24,16},{28,20},{32,24},{36,28},{40,32... | collective-permute-start | bytes 98312 | tf_op jit(solution)/shard_map/ppermute | solution.py:12
  252.6 34.9 %collective-permute-start.17 = (f32[64,128]{1,0:T(8,128)}, f32[64,128]{1,0:T(8,128)}, u32[]{:S(2)}, u32[]{:S(2)}) collective-permute-start(f32[64,128]{1,0:T(8,128)} %get-tuple-element.50), channel_id=1, source_target_pairs={{4,0},{8,4},{12,8},{16,12},{20,16},{24,20},{28,24},{32,28},{36,32}... | collective-permute-start | bytes 98312 | tf_op jit(solution)/shard_map/ppermute | solution.py:12
  259.7 34.8 %collective-permute-start.19 = (f32[64,128]{1,0:T(8,128)}, f32[64,128]{1,0:T(8,128)}, u32[]{:S(2)}, u32[]{:S(2)}) collective-permute-start(f32[64,128]{1,0:T(8,128)} %get-tuple-element.48), channel_id=1, source_target_pairs={{8,0},{12,4},{16,8},{20,12},{24,16},{28,20},{32,24},{36,28},{40,32... | collective-permute-start | bytes 98312 | tf_op jit(solution)/shard_map/ppermute | solution.py:12
  281.7 32.1 %collective-permute-start.49 = (f32[64,128]{0,1:T(8,128)}, f32[64,128]{0,1:T(8,128)S(1)}, u32[]{:S(2)}, u32[]{:S(2)}) collective-permute-start(f32[64,128]{0,1:T(8,128)} %get-tuple-element.18), channel_id=1, source_target_pairs={{4,0},{8,4},{12,8},{16,12},{20,16},{24,20},{28,24},{32,28},{36,32}... | collective-permute-start | bytes 98312 | tf_op jit(solution)/shard_map/ppermute | solution.py:12
  288.3 32.4 %collective-permute-start.51 = (f32[64,128]{0,1:T(8,128)}, f32[64,128]{0,1:T(8,128)}, u32[]{:S(2)}, u32[]{:S(2)}) collective-permute-start(f32[64,128]{0,1:T(8,128)} %get-tuple-element.16), channel_id=1, source_target_pairs={{8,0},{12,4},{16,8},{20,12},{24,16},{28,20},{32,24},{36,28},{40,32... | collective-permute-start | bytes 98312 | tf_op jit(solution)/shard_map/ppermute | solution.py:12
  307.3 34.2 %collective-permute-start.21 = (f32[64,128]{1,0:T(8,128)S(1)}, f32[64,128]{1,0:T(8,128)S(1)}, u32[]{:S(2)}, u32[]{:S(2)}) collective-permute-start(f32[64,128]{1,0:T(8,128)S(1)} %get-tuple-element.46), channel_id=1, source_target_pairs={{4,0},{8,4},{12,8},{16,12},{20,16},{24,20},{28,24},{32,28},{36,32}... | collective-permute-start | bytes 98312 | tf_op jit(solution)/shard_map/ppermute | solution.py:12
  314.4 33.0 %collective-permute-start.23 = (f32[64,128]{1,0:T(8,128)S(1)}, f32[64,128]{1,0:T(8,128)S(1)}, u32[]{:S(2)}, u32[]{:S(2)}) collective-permute-start(f32[64,128]{1,0:T(8,128)S(1)} %get-tuple-element.44), channel_id=1, source_target_pairs={{8,0},{12,4},{16,8},{20,12},{24,16},{28,20},{32,24},{36,28},{40,32... | collective-permute-start | bytes 98312 | tf_op jit(solution)/shard_map/ppermute | solution.py:12
  336.4 30.0 %collective-permute-start.53 = (f32[64,128]{0,1:T(8,128)}, f32[64,128]{0,1:T(8,128)S(1)}, u32[]{:S(2)}, u32[]{:S(2)}) collective-permute-start(f32[64,128]{0,1:T(8,128)} %get-tuple-element.14), channel_id=1, source_target_pairs={{4,0},{8,4},{12,8},{16,12},{20,16},{24,20},{28,24},{32,28},{36,32}... | collective-permute-start | bytes 98312 | tf_op jit(solution)/shard_map/ppermute | solution.py:12
  341.6 31.6 %collective-permute-start.55 = (f32[64,128]{0,1:T(8,128)}, f32[64,128]{0,1:T(8,128)}, u32[]{:S(2)}, u32[]{:S(2)}) collective-permute-start(f32[64,128]{0,1:T(8,128)} %get-tuple-element.12), channel_id=1, source_target_pairs={{8,0},{12,4},{16,8},{20,12},{24,16},{28,20},{32,24},{36,28},{40,32... | collective-permute-start | bytes 98312 | tf_op jit(solution)/shard_map/ppermute | solution.py:12
  359.9 34.9 %collective-permute-start.25 = (f32[64,128]{1,0:T(8,128)}, f32[64,128]{1,0:T(8,128)}, u32[]{:S(2)}, u32[]{:S(2)}) collective-permute-start(f32[64,128]{1,0:T(8,128)} %get-tuple-element.42), channel_id=1, source_target_pairs={{4,0},{8,4},{12,8},{16,12},{20,16},{24,20},{28,24},{32,28},{36,32}... | collective-permute-start | bytes 98312 | tf_op jit(solution)/shard_map/ppermute | solution.py:12
  367.1 34.8 %collective-permute-start.27 = (f32[64,128]{1,0:T(8,128)}, f32[64,128]{1,0:T(8,128)}, u32[]{:S(2)}, u32[]{:S(2)}) collective-permute-start(f32[64,128]{1,0:T(8,128)} %get-tuple-element.40), channel_id=1, source_target_pairs={{8,0},{12,4},{16,8},{20,12},{24,16},{28,20},{32,24},{36,28},{40,32... | collective-permute-start | bytes 98312 | tf_op jit(solution)/shard_map/ppermute | solution.py:12
  389.0 32.7 %collective-permute-start.57 = (f32[64,128]{0,1:T(8,128)}, f32[64,128]{0,1:T(8,128)S(1)}, u32[]{:S(2)}, u32[]{:S(2)}) collective-permute-start(f32[64,128]{0,1:T(8,128)} %get-tuple-element.10), channel_id=1, source_target_pairs={{4,0},{8,4},{12,8},{16,12},{20,16},{24,20},{28,24},{32,28},{36,32}... | collective-permute-start | bytes 98312 | tf_op jit(solution)/shard_map/ppermute | solution.py:12
  395.6 33.0 %collective-permute-start.59 = (f32[64,128]{0,1:T(8,128)}, f32[64,128]{0,1:T(8,128)}, u32[]{:S(2)}, u32[]{:S(2)}) collective-permute-start(f32[64,128]{0,1:T(8,128)} %get-tuple-element.8), channel_id=1, source_target_pairs={{8,0},{12,4},{16,8},{20,12},{24,16},{28,20},{32,24},{36,28},{40,32... | collective-permute-start | bytes 98312 | tf_op jit(solution)/shard_map/ppermute | solution.py:12
  415.2 34.4 %collective-permute-start.29 = (f32[64,128]{1,0:T(8,128)}, f32[64,128]{1,0:T(8,128)}, u32[]{:S(2)}, u32[]{:S(2)}) collective-permute-start(f32[64,128]{1,0:T(8,128)} %get-tuple-element.38), channel_id=1, source_target_pairs={{4,0},{8,4},{12,8},{16,12},{20,16},{24,20},{28,24},{32,28},{36,32}... | collective-permute-start | bytes 98312 | tf_op jit(solution)/shard_map/ppermute | solution.py:12
  422.4 34.4 %collective-permute-start.31 = (f32[64,128]{1,0:T(8,128)}, f32[64,128]{1,0:T(8,128)}, u32[]{:S(2)}, u32[]{:S(2)}) collective-permute-start(f32[64,128]{1,0:T(8,128)} %get-tuple-element.36), channel_id=1, source_target_pairs={{8,0},{12,4},{16,8},{20,12},{24,16},{28,20},{32,24},{36,28},{40,32... | collective-permute-start | bytes 98312 | tf_op jit(solution)/shard_map/ppermute | solution.py:12
  (49 other events, 870.0 us)
Sparse Core Ops, SparseCore 0:
  473.9 181.1 all-reduce.1
where the time goes:
time: 673 us; the launch traced here: 664 us
  waiting for transfers between devices  187 us (28%)
  starting transfers between devices  164 us (24%)
  matrix products  131 us (19%)
  local copies, waits for them, and re-layouts  127 us (19%)
  blocking collectives  26.5 us (4%)
  between operations  15.7 us (2%)
  other arithmetic  13 us (2%)
    psum x1, waiting for transfers between devices, local(): summed = lax.psum(local_grads, 'dom')  173 us
    ppermute x64, starting transfers between devices, from_behind(): return lax.ppermute(block, axis, route)  163 us
    dot_general x16, matrix products, apply_operator(): jnp.einsum('ctj,tjk->ctk', picked, tile_values, precision=lax.Precision.H...  107 us
    unnamed x82, local copies, waits for them, and re-layouts  37.6 us
    gather x16, local copies, waits for them, and re-layouts, apply_operator(): picked = jnp.take(blocks, tile_cols.reshape(-1), axis=1)  31.3 us
    gather x24, local copies, waits for them, and re-layouts, apply_operator(): outgoing = jnp.take(field_in, send_list[0], axis=1)  18 us
    concatenate x16, local copies, waits for them, and re-layouts, apply_operator(): extended = jnp.concatenate([field_in] + received, axis=1)  14.5 us
    ppermute x64, waiting for transfers between devices, from_behind(): return lax.ppermute(block, axis, route)  14 us
  transfers between devices with their start and end apart: 65, of which 4 were waited for; matrix products, arithmetic and copies ran while one was open for 36% of the time, Pallas kernels for 0%

commit v1 on v0

--- a/solution.py
+++ b/solution.py
@@ -72,7 +72,7 @@
         )
     input_grad = mixed_term(0) + operator_on(current) - clen_later
     local_grads = jnp.stack(grad_terms)
-    summed = lax.psum(local_grads, "dom")
+    summed = jnp.sum(lax.all_gather(local_grads, "dom"), axis=0)
     nodes_all = lax.axis_size("dom") * local_nodes
     return (input_grad, summed * float(nodes_all) ** (-0.5))
 

time: 673 us -> 449 us (0.67)
  waiting for transfers between devices: 187 us -> 14.9 us
  local copies, waits for them, and re-layouts: 127 us -> 70 us
  matrix products: 131 us -> 122 us
  starting transfers between devices: 164 us -> 173 us
    psum x1 -> x0, waiting for transfers between devices: 173 us -> none  [local(): summed = lax.psum(local_grads, 'dom')]
    unnamed x82 -> x72, local copies, waits for them, and re-layouts: 37.6 us -> 14.6 us
    reduce_sum x0 -> x1, other arithmetic: none -> 13.3 us  [local(): summed = jnp.sum(lax.all_gather(local_grads, 'dom'), axis=0)]
    gather x16, local copies, waits for them, and re-layouts: 31.3 us -> 18.5 us  [apply_operator(): picked = jnp.take(blocks, tile_cols.reshape(-1), axis=1)]
    dot_general x16, matrix products: 107 us -> 96.7 us  [apply_operator(): jnp.einsum('ctj,tjk->ctk', picked, tile_values, precision=lax.Precision.H...]
    concatenate x16, local copies, waits for them, and re-layouts: 14.5 us -> 4.38 us  [apply_operator(): extended = jnp.concatenate([field_in] + received, axis=1)]
    ppermute x64, starting transfers between devices: 163 us -> 173 us  [from_behind(): return lax.ppermute(block, axis, route)]
    squeeze x16, local copies, waits for them, and re-layouts: 8.17 us -> 0.25 us  [exchange_rows(): outgoing[:, slot_index]]
  transfers between devices with their start and end apart: 65 -> 65, of which waited for: 4 -> 15; matrix products, arithmetic and copies ran while one was open for 36% -> 26% of each run, Pallas kernels for 0% -> 0%
where the time goes in v1:
time: 449 us; the launch traced here: 440 us
  starting transfers between devices  173 us (39%)
  matrix products  122 us (27%)
  local copies, waits for them, and re-layouts  70 us (16%)
  blocking collectives  25.7 us (6%)
  other arithmetic  18.5 us (4%)
  between operations  16.1 us (4%)
  waiting for transfers between devices  14.9 us (3%)
    ppermute x64, starting transfers between devices, from_behind(): return lax.ppermute(block, axis, route)  173 us
    dot_general x16, matrix products, apply_operator(): jnp.einsum('ctj,tjk->ctk', picked, tile_values, precision=lax.Precision.H...  96.7 us
    gather x16, local copies, waits for them, and re-layouts, apply_operator(): picked = jnp.take(blocks, tile_cols.reshape(-1), axis=1)  18.5 us
    gather x24, local copies, waits for them, and re-layouts, apply_operator(): outgoing = jnp.take(field_in, send_list[0], axis=1)  18.3 us
    ppermute x64, waiting for transfers between devices, from_behind(): return lax.ppermute(block, axis, route)  14.9 us
    unnamed x72, local copies, waits for them, and re-layouts  14.6 us
    dot_general x9, matrix products, mixed_term(): jnp.dot(weights[order_index], cot_all, preferred_element_type=jnp.float32)  14.4 us
    reduce_sum x1, other arithmetic, local(): summed = jnp.sum(lax.all_gather(local_grads, 'dom'), axis=0)  13.3 us
  transfers between devices with their start and end apart: 65, of which 15 were waited for; matrix products, arithmetic and copies ran while one was open for 26% of the time, Pallas kernels for 0%

profile of v1, /device:TPU:2, one launch (start us, length us, event | category | flops | bytes accessed | tf_op | source)
XLA Modules:
  0.0 440.1 jit_solution(7844595746870181995)
XLA Ops:
  11.9 7.8 %collective-permute-start.33 = (f32[64,128]{0,1:T(8,128)S(1)}, f32[64,128]{0,1:T(8,128)S(1)}, u32[]{:S(2)}, u32[]{:S(2)}) collective-permute-start(f32[64,128]{0,1:T(8,128)S(1)} %get-tuple-element.34), channel_id=1, source_target_pairs={{4,0},{8,4},{12,8},{16,12},{20,16},{24,20},{28,24},{32,28},{36,32}... | collective-permute-start | bytes 98312 | tf_op jit(solution)/shard_map/ppermute | solution.py:12
  25.1 12.9 %all_gather.13 = bf16[256,1024]{1,0:T(8,128)(2,1)S(1)} all-gather(bf16[64,1024]{1,0:T(8,128)(2,1)S(1)} %copy-done.9), channel_id=1, replica_groups=mesh['dom'=64,'chan'=4] {'chan'}, dimensions={0}, use_global_device_ids=true | all-gather | bytes 655360 | tf_op jit(solution)/shard_map/all_gather | solution.py:46
  40.0 5.7 %bitcast_reduce_fusion.7 = f32[64,8,128]{2,0,1:T(8,128)S(1)} fusion(f32[64,128,128]{2,1,0:T(8,128)} %param.13, f32[64,64,128]{2,1,0:T(8,128)S(1)} %gather_fusion.17, pred[64]{0:T(512)(128)(4,1)S(1)} %compare_and_fusion), kind=kOutput, calls=%fused_computation.39 | convolution fusion | flops 806289408 | bytes 6553664 | tf_op jit(solution)/shard_map/ctj,tjk->ctk/dot_general | solution.py:32
  52.3 5.5 %collective-permute-start.39 = (f32[64,128]{0,1:T(8,128)S(1)}, f32[64,128]{0,1:T(8,128)S(1)}, u32[]{:S(2)}, u32[]{:S(2)}) collective-permute-start(f32[64,128]{0,1:T(8,128)S(1)} %get-tuple-element.28), channel_id=1, source_target_pairs={{8,0},{12,4},{16,8},{20,12},{24,16},{28,20},{32,24},{36,28},{40,32... | collective-permute-start | bytes 98312 | tf_op jit(solution)/shard_map/ppermute | solution.py:12
  60.9 5.7 %bitcast_reduce_fusion.6 = f32[64,8,128]{2,0,1:T(8,128)S(1)} fusion(f32[64,128,128]{2,1,0:T(8,128)} %param.13, f32[64,64,128]{2,1,0:T(8,128)S(1)} %gather_fusion.19, pred[64]{0:T(512)(128)(4,1)S(1)} %compare_and_fusion), kind=kOutput, calls=%fused_computation.38 | convolution fusion | flops 806289408 | bytes 6553664 | tf_op jit(solution)/shard_map/ctj,tjk->ctk/dot_general | solution.py:32
  75.1 5.3 %collective-permute-start.43 = (f32[64,128]{0,1:T(8,128)S(1)}, f32[64,128]{0,1:T(8,128)S(1)}, u32[]{:S(2)}, u32[]{:S(2)}) collective-permute-start(f32[64,128]{0,1:T(8,128)S(1)} %get-tuple-element.24), channel_id=1, source_target_pairs={{8,0},{12,4},{16,8},{20,12},{24,16},{28,20},{32,24},{36,28},{40,32... | collective-permute-start | bytes 98312 | tf_op jit(solution)/shard_map/ppermute | solution.py:12
  85.0 6.7 %bitcast_reduce_fusion.5 = f32[64,8,128]{2,0,1:T(8,128)S(1)} fusion(f32[64,128,128]{2,1,0:T(8,128)} %param.13, f32[64,64,128]{2,1,0:T(8,128)} %gather_fusion.21, pred[64]{0:T(512)(128)(4,1)S(1)} %compare_and_fusion), kind=kOutput, calls=%fused_computation.37 | convolution fusion | flops 806289408 | bytes 6553664 | tf_op jit(solution)/shard_map/ctj,tjk->ctk/dot_general | solution.py:32
  98.8 5.3 %collective-permute-start.47 = (f32[64,128]{0,1:T(8,128)S(1)}, f32[64,128]{0,1:T(8,128)S(1)}, u32[]{:S(2)}, u32[]{:S(2)}) collective-permute-start(f32[64,128]{0,1:T(8,128)S(1)} %get-tuple-element.20), channel_id=1, source_target_pairs={{8,0},{12,4},{16,8},{20,12},{24,16},{28,20},{32,24},{36,28},{40,32... | collective-permute-start | bytes 98312 | tf_op jit(solution)/shard_map/ppermute | solution.py:12
  108.7 6.7 %bitcast_reduce_fusion.4 = f32[64,8,128]{2,0,1:T(8,128)S(1)} fusion(f32[64,128,128]{2,1,0:T(8,128)} %param.13, f32[64,64,128]{2,1,0:T(8,128)} %gather_fusion.23, pred[64]{0:T(512)(128)(4,1)S(1)} %compare_and_fusion), kind=kOutput, calls=%fused_computation.36 | convolution fusion | flops 806289408 | bytes 6553664 | tf_op jit(solution)/shard_map/ctj,tjk->ctk/dot_general | solution.py:32
  122.0 5.5 %collective-permute-start.51 = (f32[64,128]{0,1:T(8,128)S(1)}, f32[64,128]{0,1:T(8,128)S(1)}, u32[]{:S(2)}, u32[]{:S(2)}) collective-permute-start(f32[64,128]{0,1:T(8,128)S(1)} %get-tuple-element.16), channel_id=1, source_target_pairs={{8,0},{12,4},{16,8},{20,12},{24,16},{28,20},{32,24},{36,28},{40,32... | collective-permute-start | bytes 98312 | tf_op jit(solution)/shard_map/ppermute | solution.py:12
  131.9 6.7 %bitcast_reduce_fusion.3 = f32[64,8,128]{2,0,1:T(8,128)S(1)} fusion(f32[64,128,128]{2,1,0:T(8,128)} %param.13, f32[64,64,128]{2,1,0:T(8,128)} %gather_fusion.25, pred[64]{0:T(512)(128)(4,1)S(1)} %compare_and_fusion), kind=kOutput, calls=%fused_computation.35 | convolution fusion | flops 806289408 | bytes 6553664 | tf_op jit(solution)/shard_map/ctj,tjk->ctk/dot_general | solution.py:32
  145.3 5.5 %collective-permute-start.55 = (f32[64,128]{0,1:T(8,128)S(1)}, f32[64,128]{0,1:T(8,128)S(1)}, u32[]{:S(2)}, u32[]{:S(2)}) collective-permute-start(f32[64,128]{0,1:T(8,128)S(1)} %get-tuple-element.12), channel_id=1, source_target_pairs={{8,0},{12,4},{16,8},{20,12},{24,16},{28,20},{32,24},{36,28},{40,32... | collective-permute-start | bytes 98312 | tf_op jit(solution)/shard_map/ppermute | solution.py:12
  155.2 6.7 %bitcast_reduce_fusion.2 = f32[64,8,128]{2,0,1:T(8,128)S(1)} fusion(f32[64,128,128]{2,1,0:T(8,128)} %param.13, f32[64,64,128]{2,1,0:T(8,128)} %gather_fusion.27, pred[64]{0:T(512)(128)(4,1)S(1)} %compare_and_fusion), kind=kOutput, calls=%fused_computation.34 | convolution fusion | flops 806289408 | bytes 6553664 | tf_op jit(solution)/shard_map/ctj,tjk->ctk/dot_general | solution.py:32
  168.6 5.7 %collective-permute-start.59 = (f32[64,128]{0,1:T(8,128)S(1)}, f32[64,128]{0,1:T(8,128)S(1)}, u32[]{:S(2)}, u32[]{:S(2)}) collective-permute-start(f32[64,128]{0,1:T(8,128)S(1)} %get-tuple-element.8), channel_id=1, source_target_pairs={{8,0},{12,4},{16,8},{20,12},{24,16},{28,20},{32,24},{36,28},{40,32... | collective-permute-start | bytes 98312 | tf_op jit(solution)/shard_map/ppermute | solution.py:12
  178.5 6.7 %bitcast_reduce_fusion.1 = f32[64,8,128]{2,0,1:T(8,128)S(1)} fusion(f32[64,128,128]{2,1,0:T(8,128)} %param.13, f32[64,64,128]{2,1,0:T(8,128)} %gather_fusion.29, pred[64]{0:T(512)(128)(4,1)S(1)} %compare_and_fusion), kind=kOutput, calls=%fused_computation.33 | convolution fusion | flops 806289408 | bytes 6553664 | tf_op jit(solution)/shard_map/ctj,tjk->ctk/dot_general | solution.py:32
  191.9 5.5 %collective-permute-start.63 = (f32[64,128]{0,1:T(8,128)S(1)}, f32[64,128]{0,1:T(8,128)S(1)}, u32[]{:S(2)}, u32[]{:S(2)}) collective-permute-start(f32[64,128]{0,1:T(8,128)S(1)} %get-tuple-element.4), channel_id=1, source_target_pairs={{8,0},{12,4},{16,8},{20,12},{24,16},{28,20},{32,24},{36,28},{40,32... | collective-permute-start | bytes 98312 | tf_op jit(solution)/shard_map/ppermute | solution.py:12
  200.4 5.7 %bitcast_reduce_fusion = f32[64,8,128]{2,0,1:T(8,128)S(1)} fusion(f32[64,128,128]{2,1,0:T(8,128)} %param.13, f32[64,64,128]{2,1,0:T(8,128)S(1)} %gather_fusion.31, pred[64]{0:T(512)(128)(4,1)S(1)} %compare_and_fusion), kind=kOutput, calls=%fused_computation.32 | convolution fusion | flops 806289408 | bytes 6553664 | tf_op jit(solution)/shard_map/ctj,tjk->ctk/dot_general | solution.py:32
  207.7 12.8 %all_gather.12 = bf16[256,1024]{1,0:T(8,128)(2,1)S(1)} all-gather(bf16[64,1024]{1,0:T(8,128)(2,1)S(1)} %copy-done.7), channel_id=1, replica_groups=mesh['dom'=64,'chan'=4] {'chan'}, dimensions={0}, use_global_device_ids=true | all-gather | bytes 655360 | tf_op jit(solution)/shard_map/all_gather | solution.py:47
  228.0 5.3 %collective-permute-start.3 = (f32[64,128]{1,0:T(8,128)S(1)}, f32[64,128]{1,0:T(8,128)S(1)}, u32[]{:S(2)}, u32[]{:S(2)}) collective-permute-start(f32[64,128]{1,0:T(8,128)S(1)} %get-tuple-element.64), channel_id=1, source_target_pairs={{8,0},{12,4},{16,8},{20,12},{24,16},{28,20},{32,24},{36,28},{40,32... | collective-permute-start | bytes 98312 | tf_op jit(solution)/shard_map/ppermute | solution.py:12
  236.5 5.7 %bitcast_reduce_fusion.15 = f32[64,8,128]{2,0,1:T(8,128)S(1)} fusion(f32[64,128,128]{2,1,0:T(8,128)} %param.13, f32[64,64,128]{2,1,0:T(8,128)S(1)} %gather_fusion.1, pred[64]{0:T(512)(128)(4,1)S(1)} %compare_and_fusion), kind=kOutput, calls=%fused_computation.47 | convolution fusion | flops 806289408 | bytes 6553664 | tf_op jit(solution)/shard_map/ctj,tjk->ctk/dot_general | solution.py:32
  261.2 5.7 %bitcast_reduce_fusion.14 = f32[64,8,128]{2,0,1:T(8,128)S(1)} fusion(f32[64,128,128]{2,1,0:T(8,128)} %param.13, f32[64,64,128]{2,1,0:T(8,128)S(1)} %gather_fusion.3, pred[64]{0:T(512)(128)(4,1)S(1)} %compare_and_fusion), kind=kOutput, calls=%fused_computation.46 | convolution fusion | flops 806289408 | bytes 6553664 | tf_op jit(solution)/shard_map/ctj,tjk->ctk/dot_general | solution.py:32
  275.2 5.3 %collective-permute-start.11 = (f32[64,128]{1,0:T(8,128)S(1)}, f32[64,128]{1,0:T(8,128)S(1)}, u32[]{:S(2)}, u32[]{:S(2)}) collective-permute-start(f32[64,128]{1,0:T(8,128)S(1)} %get-tuple-element.56), channel_id=1, source_target_pairs={{8,0},{12,4},{16,8},{20,12},{24,16},{28,20},{32,24},{36,28},{40,32... | collective-permute-start | bytes 98312 | tf_op jit(solution)/shard_map/ppermute | solution.py:12
  286.2 6.1 %bitcast_reduce_fusion.13 = f32[64,8,128]{2,0,1:T(8,128)S(1)} fusion(f32[64,128,128]{2,1,0:T(8,128)} %param.13, f32[64,64,128]{2,1,0:T(8,128)S(1)} %gather_fusion.5, pred[64]{0:T(512)(128)(4,1)S(1)} %compare_and_fusion), kind=kOutput, calls=%fused_computation.45 | convolution fusion | flops 806289408 | bytes 6553664 | tf_op jit(solution)/shard_map/ctj,tjk->ctk/dot_general | solution.py:32
  311.9 5.7 %bitcast_reduce_fusion.12 = f32[64,8,128]{2,0,1:T(8,128)S(1)} fusion(f32[64,128,128]{2,1,0:T(8,128)} %param.13, f32[64,64,128]{2,1,0:T(8,128)S(1)} %gather_fusion.7, pred[64]{0:T(512)(128)(4,1)S(1)} %compare_and_fusion), kind=kOutput, calls=%fused_computation.44 | convolution fusion | flops 806289408 | bytes 6553664 | tf_op jit(solution)/shard_map/ctj,tjk->ctk/dot_general | solution.py:32
  325.9 5.3 %collective-permute-start.19 = (f32[64,128]{1,0:T(8,128)S(1)}, f32[64,128]{1,0:T(8,128)S(1)}, u32[]{:S(2)}, u32[]{:S(2)}) collective-permute-start(f32[64,128]{1,0:T(8,128)S(1)} %get-tuple-element.48), channel_id=1, source_target_pairs={{8,0},{12,4},{16,8},{20,12},{24,16},{28,20},{32,24},{36,28},{40,32... | collective-permute-start | bytes 98312 | tf_op jit(solution)/shard_map/ppermute | solution.py:12
  337.0 5.7 %bitcast_reduce_fusion.11 = f32[64,8,128]{2,0,1:T(8,128)S(1)} fusion(f32[64,128,128]{2,1,0:T(8,128)} %param.13, f32[64,64,128]{2,1,0:T(8,128)S(1)} %gather_fusion.9, pred[64]{0:T(512)(128)(4,1)S(1)} %compare_and_fusion), kind=kOutput, calls=%fused_computation.43 | convolution fusion | flops 806289408 | bytes 6553664 | tf_op jit(solution)/shard_map/ctj,tjk->ctk/dot_general | solution.py:32
  351.0 5.6 %collective-permute-start.23 = (f32[64,128]{1,0:T(8,128)S(1)}, f32[64,128]{1,0:T(8,128)S(1)}, u32[]{:S(2)}, u32[]{:S(2)}) collective-permute-start(f32[64,128]{1,0:T(8,128)S(1)} %get-tuple-element.44), channel_id=1, source_target_pairs={{8,0},{12,4},{16,8},{20,12},{24,16},{28,20},{32,24},{36,28},{40,32... | collective-permute-start | bytes 98312 | tf_op jit(solution)/shard_map/ppermute | solution.py:12
  362.1 6.0 %bitcast_reduce_fusion.10 = f32[64,8,128]{2,0,1:T(8,128)S(1)} fusion(f32[64,128,128]{2,1,0:T(8,128)} %param.13, f32[64,64,128]{2,1,0:T(8,128)S(1)} %gather_fusion.11, pred[64]{0:T(512)(128)(4,1)S(1)} %compare_and_fusion), kind=kOutput, calls=%fused_computation.42 | convolution fusion | flops 806289408 | bytes 6553664 | tf_op jit(solution)/shard_map/ctj,tjk->ctk/dot_general | solution.py:32
  386.9 5.7 %bitcast_reduce_fusion.9 = f32[64,8,128]{2,0,1:T(8,128)S(1)} fusion(f32[64,128,128]{2,1,0:T(8,128)} %param.13, f32[64,64,128]{2,1,0:T(8,128)S(1)} %gather_fusion.13, pred[64]{0:T(512)(128)(4,1)S(1)} %compare_and_fusion), kind=kOutput, calls=%fused_computation.41 | convolution fusion | flops 806289408 | bytes 6553664 | tf_op jit(solution)/shard_map/ctj,tjk->ctk/dot_general | solution.py:32
  400.9 5.6 %collective-permute-start.31 = (f32[64,128]{1,0:T(8,128)S(1)}, f32[64,128]{1,0:T(8,128)S(1)}, u32[]{:S(2)}, u32[]{:S(2)}) collective-permute-start(f32[64,128]{1,0:T(8,128)S(1)} %get-tuple-element.36), channel_id=1, source_target_pairs={{8,0},{12,4},{16,8},{20,12},{24,16},{28,20},{32,24},{36,28},{40,32... | collective-permute-start | bytes 98312 | tf_op jit(solution)/shard_map/ppermute | solution.py:12
  411.2 5.7 %bitcast_reduce_fusion.8 = f32[64,8,128]{2,0,1:T(8,128)S(1)} fusion(f32[64,128,128]{2,1,0:T(8,128)} %param.13, f32[64,64,128]{2,1,0:T(8,128)S(1)} %gather_fusion.15, pred[64]{0:T(512)(128)(4,1)S(1)} %compare_and_fusion), kind=kOutput, calls=%fused_computation.40 | convolution fusion | flops 806289408 | bytes 6553664 | tf_op jit(solution)/shard_map/ctj,tjk->ctk/dot_general | solution.py:32
  418.6 13.3 %reduce_sum.169 = f32[9,256,64]{1,2,0:T(8,128)S(1)} reduce(f32[64,9,256,64]{2,3,1,0:T(8,128)} %bitcast.586, f32[]{:T(128)} %constant.19.clone.1), dimensions={0}, to_apply=%region_16.19 | reduce | flops 9289728 | bytes 38338564 | tf_op jit(solution)/shard_map/reduce_sum | solution.py:75
  (351 shorter events, 214.7 us)
Async XLA Ops:
  7.2 411.4 %all-gather.3.cloned.1.call-start = ((), (), s32[]{:S(2)}) async-start(), calls=%async_computation | async-start | bytes 38338560 | tf_op jit(solution)/shard_map/all_gather | solution.py:75
  11.8 27.2 %collective-permute-start.32 = (f32[64,128]{0,1:T(8,128)S(1)}, f32[64,128]{0,1:T(8,128)S(1)}, u32[]{:S(2)}, u32[]{:S(2)}) collective-permute-start(f32[64,128]{0,1:T(8,128)S(1)} %get-tuple-element.35), channel_id=1, source_target_pairs={{252,0},{0,4},{4,8},{8,12},{12,16},{16,20},{20,24},{24,28},{28,32}... | collective-permute-start | bytes 98312 | tf_op jit(solution)/shard_map/ppermute | solution.py:12
  11.9 27.1 %collective-permute-start.33 = (f32[64,128]{0,1:T(8,128)S(1)}, f32[64,128]{0,1:T(8,128)S(1)}, u32[]{:S(2)}, u32[]{:S(2)}) collective-permute-start(f32[64,128]{0,1:T(8,128)S(1)} %get-tuple-element.34), channel_id=1, source_target_pairs={{4,0},{8,4},{12,8},{16,12},{20,16},{24,20},{28,24},{32,28},{36,32}... | collective-permute-start | bytes 98312 | tf_op jit(solution)/shard_map/ppermute | solution.py:12
  19.7 19.3 %collective-permute-start.34 = (f32[64,128]{0,1:T(8,128)S(1)}, f32[64,128]{0,1:T(8,128)S(1)}, u32[]{:S(2)}, u32[]{:S(2)}) collective-permute-start(f32[64,128]{0,1:T(8,128)S(1)} %get-tuple-element.33), channel_id=1, source_target_pairs={{248,0},{252,4},{0,8},{4,12},{8,16},{12,20},{16,24},{20,28},{24,32... | collective-permute-start | bytes 98312 | tf_op jit(solution)/shard_map/ppermute | solution.py:12
  19.7 19.3 %collective-permute-start.35 = (f32[64,128]{0,1:T(8,128)S(1)}, f32[64,128]{0,1:T(8,128)S(1)}, u32[]{:S(2)}, u32[]{:S(2)}) collective-permute-start(f32[64,128]{0,1:T(8,128)S(1)} %get-tuple-element.32), channel_id=1, source_target_pairs={{8,0},{12,4},{16,8},{20,12},{24,16},{28,20},{32,24},{36,28},{40,32... | collective-permute-start | bytes 98312 | tf_op jit(solution)/shard_map/ppermute | solution.py:12
  47.1 11.9 %collective-permute-start.36 = (f32[64,128]{0,1:T(8,128)S(1)}, f32[64,128]{0,1:T(8,128)S(1)}, u32[]{:S(2)}, u32[]{:S(2)}) collective-permute-start(f32[64,128]{0,1:T(8,128)S(1)} %get-tuple-element.31), channel_id=1, source_target_pairs={{252,0},{0,4},{4,8},{8,12},{12,16},{16,20},{20,24},{24,28},{28,32}... | collective-permute-start | bytes 98312 | tf_op jit(solution)/shard_map/ppermute | solution.py:12
  47.2 11.9 %collective-permute-start.37 = (f32[64,128]{0,1:T(8,128)S(1)}, f32[64,128]{0,1:T(8,128)S(1)}, u32[]{:S(2)}, u32[]{:S(2)}) collective-permute-start(f32[64,128]{0,1:T(8,128)S(1)} %get-tuple-element.30), channel_id=1, source_target_pairs={{4,0},{8,4},{12,8},{16,12},{20,16},{24,20},{28,24},{32,28},{36,32}... | collective-permute-start | bytes 98312 | tf_op jit(solution)/shard_map/ppermute | solution.py:12
  69.9 11.7 %collective-permute-start.40 = (f32[64,128]{0,1:T(8,128)S(1)}, f32[64,128]{0,1:T(8,128)S(1)}, u32[]{:S(2)}, u32[]{:S(2)}) collective-permute-start(f32[64,128]{0,1:T(8,128)S(1)} %get-tuple-element.27), channel_id=1, source_target_pairs={{252,0},{0,4},{4,8},{8,12},{12,16},{16,20},{20,24},{24,28},{28,32}... | collective-permute-start | bytes 98312 | tf_op jit(solution)/shard_map/ppermute | solution.py:12
  70.0 11.6 %collective-permute-start.41 = (f32[64,128]{0,1:T(8,128)S(1)}, f32[64,128]{0,1:T(8,128)S(1)}, u32[]{:S(2)}, u32[]{:S(2)}) collective-permute-start(f32[64,128]{0,1:T(8,128)S(1)} %get-tuple-element.26), channel_id=1, source_target_pairs={{4,0},{8,4},{12,8},{16,12},{20,16},{24,20},{28,24},{32,28},{36,32}... | collective-permute-start | bytes 98312 | tf_op jit(solution)/shard_map/ppermute | solution.py:12
  93.2 12.1 %collective-permute-start.44 = (f32[64,128]{0,1:T(8,128)S(1)}, f32[64,128]{0,1:T(8,128)S(1)}, u32[]{:S(2)}, u32[]{:S(2)}) collective-permute-start(f32[64,128]{0,1:T(8,128)S(1)} %get-tuple-element.23), channel_id=1, source_target_pairs={{252,0},{0,4},{4,8},{8,12},{12,16},{16,20},{20,24},{24,28},{28,32}... | collective-permute-start | bytes 98312 | tf_op jit(solution)/shard_map/ppermute | solution.py:12
  93.7 11.6 %collective-permute-start.45 = (f32[64,128]{0,1:T(8,128)S(1)}, f32[64,128]{0,1:T(8,128)S(1)}, u32[]{:S(2)}, u32[]{:S(2)}) collective-permute-start(f32[64,128]{0,1:T(8,128)S(1)} %get-tuple-element.22), channel_id=1, source_target_pairs={{4,0},{8,4},{12,8},{16,12},{20,16},{24,20},{28,24},{32,28},{36,32}... | collective-permute-start | bytes 98312 | tf_op jit(solution)/shard_map/ppermute | solution.py:12
  116.9 11.9 %collective-permute-start.48 = (f32[64,128]{0,1:T(8,128)S(1)}, f32[64,128]{0,1:T(8,128)S(1)}, u32[]{:S(2)}, u32[]{:S(2)}) collective-permute-start(f32[64,128]{0,1:T(8,128)S(1)} %get-tuple-element.19), channel_id=1, source_target_pairs={{252,0},{0,4},{4,8},{8,12},{12,16},{16,20},{20,24},{24,28},{28,32}... | collective-permute-start | bytes 98312 | tf_op jit(solution)/shard_map/ppermute | solution.py:12
  117.0 11.8 %collective-permute-start.49 = (f32[64,128]{0,1:T(8,128)S(1)}, f32[64,128]{0,1:T(8,128)S(1)}, u32[]{:S(2)}, u32[]{:S(2)}) collective-permute-start(f32[64,128]{0,1:T(8,128)S(1)} %get-tuple-element.18), channel_id=1, source_target_pairs={{4,0},{8,4},{12,8},{16,12},{20,16},{24,20},{28,24},{32,28},{36,32}... | collective-permute-start | bytes 98312 | tf_op jit(solution)/shard_map/ppermute | solution.py:12
  140.2 11.9 %collective-permute-start.52 = (f32[64,128]{0,1:T(8,128)S(1)}, f32[64,128]{0,1:T(8,128)S(1)}, u32[]{:S(2)}, u32[]{:S(2)}) collective-permute-start(f32[64,128]{0,1:T(8,128)S(1)} %get-tuple-element.15), channel_id=1, source_target_pairs={{252,0},{0,4},{4,8},{8,12},{12,16},{16,20},{20,24},{24,28},{28,32}... | collective-permute-start | bytes 98312 | tf_op jit(solution)/shard_map/ppermute | solution.py:12
  140.2 11.8 %collective-permute-start.53 = (f32[64,128]{0,1:T(8,128)S(1)}, f32[64,128]{0,1:T(8,128)S(1)}, u32[]{:S(2)}, u32[]{:S(2)}) collective-permute-start(f32[64,128]{0,1:T(8,128)S(1)} %get-tuple-element.14), channel_id=1, source_target_pairs={{4,0},{8,4},{12,8},{16,12},{20,16},{24,20},{28,24},{32,28},{36,32}... | collective-permute-start | bytes 98312 | tf_op jit(solution)/shard_map/ppermute | solution.py:12
  163.4 12.1 %collective-permute-start.56 = (f32[64,128]{0,1:T(8,128)S(1)}, f32[64,128]{0,1:T(8,128)S(1)}, u32[]{:S(2)}, u32[]{:S(2)}) collective-permute-start(f32[64,128]{0,1:T(8,128)S(1)} %get-tuple-element.11), channel_id=1, source_target_pairs={{252,0},{0,4},{4,8},{8,12},{12,16},{16,20},{20,24},{24,28},{28,32}... | collective-permute-start | bytes 98312 | tf_op jit(solution)/shard_map/ppermute | solution.py:12
  163.5 12.0 %collective-permute-start.57 = (f32[64,128]{0,1:T(8,128)S(1)}, f32[64,128]{0,1:T(8,128)S(1)}, u32[]{:S(2)}, u32[]{:S(2)}) collective-permute-start(f32[64,128]{0,1:T(8,128)S(1)} %get-tuple-element.10), channel_id=1, source_target_pairs={{4,0},{8,4},{12,8},{16,12},{20,16},{24,20},{28,24},{32,28},{36,32}... | collective-permute-start | bytes 98312 | tf_op jit(solution)/shard_map/ppermute | solution.py:12
  186.7 11.9 %collective-permute-start.60 = (f32[64,128]{0,1:T(8,128)S(1)}, f32[64,128]{0,1:T(8,128)S(1)}, u32[]{:S(2)}, u32[]{:S(2)}) collective-permute-start(f32[64,128]{0,1:T(8,128)S(1)} %get-tuple-element.7), channel_id=1, source_target_pairs={{252,0},{0,4},{4,8},{8,12},{12,16},{16,20},{20,24},{24,28},{28,32}... | collective-permute-start | bytes 98312 | tf_op jit(solution)/shard_map/ppermute | solution.py:12
  186.8 11.8 %collective-permute-start.61 = (f32[64,128]{0,1:T(8,128)S(1)}, f32[64,128]{0,1:T(8,128)S(1)}, u32[]{:S(2)}, u32[]{:S(2)}) collective-permute-start(f32[64,128]{0,1:T(8,128)S(1)} %get-tuple-element.6), channel_id=1, source_target_pairs={{4,0},{8,4},{12,8},{16,12},{20,16},{24,20},{28,24},{32,28},{36,32}... | collective-permute-start | bytes 98312 | tf_op jit(solution)/shard_map/ppermute | solution.py:12
  222.9 10.5 %collective-permute-start = (f32[64,128]{1,0:T(8,128)S(1)}, f32[64,128]{1,0:T(8,128)S(1)}, u32[]{:S(2)}, u32[]{:S(2)}) collective-permute-start(f32[64,128]{1,0:T(8,128)S(1)} %get-tuple-element.67), channel_id=1, source_target_pairs={{252,0},{0,4},{4,8},{8,12},{12,16},{16,20},{20,24},{24,28},{28,32}... | collective-permute-start | bytes 98312 | tf_op jit(solution)/shard_map/ppermute | solution.py:12
  245.3 10.9 %collective-permute-start.4 = (f32[64,128]{1,0:T(8,128)S(1)}, f32[64,128]{1,0:T(8,128)S(1)}, u32[]{:S(2)}, u32[]{:S(2)}) collective-permute-start(f32[64,128]{1,0:T(8,128)S(1)} %get-tuple-element.63), channel_id=1, source_target_pairs={{252,0},{0,4},{4,8},{8,12},{12,16},{16,20},{20,24},{24,28},{28,32}... | collective-permute-start | bytes 98312 | tf_op jit(solution)/shard_map/ppermute | solution.py:12
  245.4 11.4 %collective-permute-start.5 = (f32[64,128]{1,0:T(8,128)S(1)}, f32[64,128]{1,0:T(8,128)S(1)}, u32[]{:S(2)}, u32[]{:S(2)}) collective-permute-start(f32[64,128]{1,0:T(8,128)S(1)} %get-tuple-element.62), channel_id=1, source_target_pairs={{4,0},{8,4},{12,8},{16,12},{20,16},{24,20},{28,24},{32,28},{36,32}... | collective-permute-start | bytes 98312 | tf_op jit(solution)/shard_map/ppermute | solution.py:12
  270.1 10.5 %collective-permute-start.8 = (f32[64,128]{1,0:T(8,128)S(1)}, f32[64,128]{1,0:T(8,128)S(1)}, u32[]{:S(2)}, u32[]{:S(2)}) collective-permute-start(f32[64,128]{1,0:T(8,128)S(1)} %get-tuple-element.59), channel_id=1, source_target_pairs={{252,0},{0,4},{4,8},{8,12},{12,16},{16,20},{20,24},{24,28},{28,32}... | collective-permute-start | bytes 98312 | tf_op jit(solution)/shard_map/ppermute | solution.py:12
  270.2 11.0 %collective-permute-start.9 = (f32[64,128]{1,0:T(8,128)S(1)}, f32[64,128]{1,0:T(8,128)S(1)}, u32[]{:S(2)}, u32[]{:S(2)}) collective-permute-start(f32[64,128]{1,0:T(8,128)S(1)} %get-tuple-element.58), channel_id=1, source_target_pairs={{4,0},{8,4},{12,8},{16,12},{20,16},{24,20},{28,24},{32,28},{36,32}... | collective-permute-start | bytes 98312 | tf_op jit(solution)/shard_map/ppermute | solution.py:12
  295.6 10.6 %collective-permute-start.12 = (f32[64,128]{1,0:T(8,128)S(1)}, f32[64,128]{1,0:T(8,128)S(1)}, u32[]{:S(2)}, u32[]{:S(2)}) collective-permute-start(f32[64,128]{1,0:T(8,128)S(1)} %get-tuple-element.55), channel_id=1, source_target_pairs={{252,0},{0,4},{4,8},{8,12},{12,16},{16,20},{20,24},{24,28},{28,32}... | collective-permute-start | bytes 98312 | tf_op jit(solution)/shard_map/ppermute | solution.py:12
  295.7 11.2 %collective-permute-start.13 = (f32[64,128]{1,0:T(8,128)S(1)}, f32[64,128]{1,0:T(8,128)S(1)}, u32[]{:S(2)}, u32[]{:S(2)}) collective-permute-start(f32[64,128]{1,0:T(8,128)S(1)} %get-tuple-element.54), channel_id=1, source_target_pairs={{4,0},{8,4},{12,8},{16,12},{20,16},{24,20},{28,24},{32,28},{36,32}... | collective-permute-start | bytes 98312 | tf_op jit(solution)/shard_map/ppermute | solution.py:12
  320.9 11.0 %collective-permute-start.17 = (f32[64,128]{1,0:T(8,128)S(1)}, f32[64,128]{1,0:T(8,128)S(1)}, u32[]{:S(2)}, u32[]{:S(2)}) collective-permute-start(f32[64,128]{1,0:T(8,128)S(1)} %get-tuple-element.50), channel_id=1, source_target_pairs={{4,0},{8,4},{12,8},{16,12},{20,16},{24,20},{28,24},{32,28},{36,32}... | collective-permute-start | bytes 98312 | tf_op jit(solution)/shard_map/ppermute | solution.py:12
  345.9 10.7 %collective-permute-start.20 = (f32[64,128]{1,0:T(8,128)S(1)}, f32[64,128]{1,0:T(8,128)S(1)}, u32[]{:S(2)}, u32[]{:S(2)}) collective-permute-start(f32[64,128]{1,0:T(8,128)S(1)} %get-tuple-element.47), channel_id=1, source_target_pairs={{252,0},{0,4},{4,8},{8,12},{12,16},{16,20},{20,24},{24,28},{28,32}... | collective-permute-start | bytes 98312 | tf_op jit(solution)/shard_map/ppermute | solution.py:12
  346.0 11.3 %collective-permute-start.21 = (f32[64,128]{1,0:T(8,128)S(1)}, f32[64,128]{1,0:T(8,128)S(1)}, u32[]{:S(2)}, u32[]{:S(2)}) collective-permute-start(f32[64,128]{1,0:T(8,128)S(1)} %get-tuple-element.46), channel_id=1, source_target_pairs={{4,0},{8,4},{12,8},{16,12},{20,16},{24,20},{28,24},{32,28},{36,32}... | collective-permute-start | bytes 98312 | tf_op jit(solution)/shard_map/ppermute | solution.py:12
  371.5 11.0 %collective-permute-start.25 = (f32[64,128]{1,0:T(8,128)S(1)}, f32[64,128]{1,0:T(8,128)S(1)}, u32[]{:S(2)}, u32[]{:S(2)}) collective-permute-start(f32[64,128]{1,0:T(8,128)S(1)} %get-tuple-element.42), channel_id=1, source_target_pairs={{4,0},{8,4},{12,8},{16,12},{20,16},{24,20},{28,24},{32,28},{36,32}... | collective-permute-start | bytes 98312 | tf_op jit(solution)/shard_map/ppermute | solution.py:12
  395.8 10.7 %collective-permute-start.28 = (f32[64,128]{1,0:T(8,128)S(1)}, f32[64,128]{1,0:T(8,128)S(1)}, u32[]{:S(2)}, u32[]{:S(2)}) collective-permute-start(f32[64,128]{1,0:T(8,128)S(1)} %get-tuple-element.39), channel_id=1, source_target_pairs={{252,0},{0,4},{4,8},{8,12},{12,16},{16,20},{20,24},{24,28},{28,32}... | collective-permute-start | bytes 98312 | tf_op jit(solution)/shard_map/ppermute | solution.py:12
  395.9 11.3 %collective-permute-start.29 = (f32[64,128]{1,0:T(8,128)S(1)}, f32[64,128]{1,0:T(8,128)S(1)}, u32[]{:S(2)}, u32[]{:S(2)}) collective-permute-start(f32[64,128]{1,0:T(8,128)S(1)} %get-tuple-element.38), channel_id=1, source_target_pairs={{4,0},{8,4},{12,8},{16,12},{20,16},{24,20},{28,24},{32,28},{36,32}... | collective-permute-start | bytes 98312 | tf_op jit(solution)/shard_map/ppermute | solution.py:12
  (44 other events, 846.2 us)
Sparse Core Ops, SparseCore 0:
  207.8 156.8 all-gather.2
